TPU v7x, 32 devices: a whole 2x2x4 slice. The times are simulated.
32 devices in a mesh: blen: 4 (over z), tm: 8 (over y, x, core).
Axes of the slice: x: 2, y: 2, z: 4, core: 2. Of those that a mesh axis runs over, the one named last changes fastest.
Arguments:
- model_grid: bfloat16 [256, 2, 512, 512], P(('blen', 'tm')), may hold values from -6 to 6
- vis_values: float32 [2, 16384], P(None, ('blen', 'tm')), may hold values from -6 to 6
- weights: float32 [16384], P(('blen', 'tm')), may hold values from 0.3 to 3
- flags: int32 [16384], P(('blen', 'tm')), may hold values 0 or 1
- uv_frac: float32 [2, 16384], P(None, ('blen', 'tm')), may hold values from 0 to 1
- cell_offset: int32 [2, 16384], P(None, ('blen', 'tm')), may hold values from 3 to 507
- tile_index: int32 [16384, 1], P(('blen', 'tm')), may hold values from 0 to 255; in each aligned block of 512 rows (0 to 511, 512 to 1023, ...) at most 4 rows name the same one
Outputs:
- gradient: float32 [8192, 8192], P(('blen', 'tm'))
- weighted_residual: float32 [2, 16384], P(None, ('blen', 'tm'))
Inputs may be any that keep to these rules, and one draw needn't show every extreme that they name: `tile_index`: in the rows of one device no tile is named by more than 4 rows, and some device has a tile named by exactly 4 rows.
All inputs are finite; a program needn't handle non-finite values. No bound on the sum of `flags` on one device may be relied on, other than what follows from the above.
Results may differ from a plain program's by a relative error of at most 0.0095.
Values sent between devices are 32-bit elements; how exact they have to be, the bound alone decides.
No kernel may reach another device: no remote copies, remote signals or barrier semaphores. Data moves between devices by JAX's collectives and lax.ppermute only.
A program may use at most 192 MiB of HBM per device.

v0:
```python
import math
import jax
import jax.numpy as jnp
from jax import lax
from jax.sharding import PartitionSpec as P

NPIX = 8192
KSUP = 8
NT = 16
MOST = 4
kernel_scale = 0.5
highest = lax.Precision.HIGHEST


def taps_full(offsets, fractions, tile_side):
    cell_ids = lax.broadcasted_iota(jnp.int32, offsets.shape + (tile_side,), offsets.ndim)
    shifted = cell_ids - offsets[..., None]
    distance = shifted.astype(jnp.float32) - fractions[..., None]
    inside = (shifted >= 1 - KSUP // 2) & (shifted <= KSUP // 2)
    values = jnp.exp(-kernel_scale * distance * distance)
    return jnp.where(inside, values, 0.0).astype(jnp.bfloat16)


def phase_table(row_count, col_count, period):
    row_ids = lax.broadcasted_iota(jnp.int32, (row_count, col_count), 0)
    col_ids = lax.broadcasted_iota(jnp.int32, (row_count, col_count), 1)
    angles = 2.0 * math.pi / period * (row_ids * col_ids % period).astype(jnp.float32)
    return (jnp.cos(angles), jnp.sin(angles))


def complex_block(cos_part, sin_part):
    return jnp.stack([jnp.stack([cos_part, -sin_part]), jnp.stack([sin_part, cos_part])])


def on_device(model_grid, vis_values, weights, flags, uv_frac, cell_offset, tile_index):
    blen_size = lax.axis_size("blen")
    tm_size = lax.axis_size("tm")
    devices = blen_size * tm_size
    per_dev = model_grid.shape[0]
    tile_side = model_grid.shape[2]
    vis_count = weights.shape[0]
    ntiles = per_dev * devices
    total_slots = ntiles * MOST
    tile_ids = tile_index[:, 0]
    matches = tile_ids[:, None] == lax.broadcasted_iota(jnp.int32, (vis_count, ntiles), 1)
    counts = jnp.sum(matches.astype(jnp.int32), axis=0)
    starts = jnp.cumsum(counts) - counts
    sorting = jnp.argsort(tile_ids, stable=True)
    position = (
        jnp.zeros((vis_count,), jnp.int32).at[sorting].set(jnp.arange(vis_count, dtype=jnp.int32))
    )
    first_slot = jnp.sum(jnp.where(matches, starts[None, :], 0), axis=1)
    rank_in_tile = position - first_slot
    owner_dev = tile_ids // per_dev
    local_tile = tile_ids % per_dev
    slot_of = (local_tile * devices + owner_dev) * MOST + rank_in_tile
    weighted = weights * flags.astype(jnp.float32)
    float_fields = jnp.stack([vis_values[0], vis_values[1], weighted, uv_frac[0], uv_frac[1]])
    send_float = jnp.zeros((5, total_slots), jnp.float32).at[:, slot_of].set(float_fields)
    send_int = jnp.zeros((2, total_slots), jnp.int32).at[:, slot_of].set(cell_offset)
    recv_float, recv_int = (
        lax.all_to_all(
            send_float.reshape(5, per_dev, devices, MOST),
            ("blen", "tm"),
            split_axis=2,
            concat_axis=2,
            tiled=True,
        ),
        lax.all_to_all(
            send_int.reshape(2, per_dev, devices, MOST),
            ("blen", "tm"),
            split_axis=2,
            concat_axis=2,
            tiled=True,
        ),
    )
    owner_rows = devices * MOST
    block_rows = 512 if owner_rows % 512 == 0 else owner_rows
    block_count = owner_rows // block_rows
    float_blocks = recv_float.reshape(5, per_dev, block_count, block_rows).transpose(2, 0, 1, 3)
    int_blocks = recv_int.reshape(2, per_dev, block_count, block_rows).transpose(2, 0, 1, 3)

    def grid_step(adjoint, inputs):
        part_float, part_int = inputs
        taps_u = taps_full(part_int[0], part_float[3], tile_side)
        taps_v = taps_full(part_int[1], part_float[4], tile_side)
        partial_sums = jnp.einsum(
            "qrj,qcji->qrci", taps_v, model_grid, preferred_element_type=jnp.float32
        )
        predicted = jnp.sum(partial_sums * taps_u[:, :, None, :], axis=-1)
        observed = jnp.stack([part_float[0], part_float[1]], axis=-1)
        residual = part_float[2][..., None] * (predicted - observed)
        spread = (residual[..., None] * taps_u[:, :, None, :]).astype(jnp.bfloat16)
        adjoint = adjoint + jnp.einsum(
            "qrj,qrci->qcji", taps_v, spread, preferred_element_type=jnp.float32
        )
        return (adjoint, jnp.moveaxis(residual, -1, 0))

    start_adjoint = jnp.zeros((per_dev, 2, tile_side, tile_side), jnp.float32)
    adjoint, residual_blocks = lax.scan(grid_step, start_adjoint, (float_blocks, int_blocks))
    residual_slots = residual_blocks.transpose(1, 2, 0, 3).reshape(2, per_dev, owner_rows)
    returned = lax.all_to_all(
        residual_slots.reshape(2, per_dev, devices, MOST),
        ("blen", "tm"),
        split_axis=2,
        concat_axis=2,
        tiled=True,
    )
    weighted_residual = returned.reshape(2, total_slots)[:, slot_of]
    relaid = lax.all_to_all(adjoint, "tm", split_axis=2, concat_axis=0, tiled=True)
    tile_cols = NT // blen_size
    col_slice = tile_side // tm_size
    pieces = relaid.reshape(NT, tile_cols, 2, col_slice, tile_side)
    cos_small, sin_small = phase_table(NT, NT, NT)
    small_turn = complex_block(cos_small, sin_small)
    cos_twist, sin_twist = phase_table(NT, tile_side, NPIX)
    cos_tile, sin_tile = phase_table(tile_side, tile_side, tile_side)
    tile_turn = complex_block(cos_tile, sin_tile)
    section_one = jnp.einsum("acnt,tvcji->anvji", small_turn, pieces, precision=highest)
    twist_c = cos_twist[:, None, None, :]
    twist_s = sin_twist[:, None, None, :]
    turned = jnp.stack(
        [
            section_one[0] * twist_c - section_one[1] * twist_s,
            section_one[0] * twist_s + section_one[1] * twist_c,
        ]
    )
    columns = jnp.einsum("acmi,cnvji->amnvj", tile_turn, turned, precision=highest)
    rows_dev = NPIX // devices
    spread_cols = rows_dev * tile_cols * col_slice
    packed = columns.reshape(2, 1, devices, spread_cols)
    landed = lax.all_to_all(packed, ("blen", "tm"), split_axis=2, concat_axis=1, tiled=True)
    landed = landed.reshape(2, blen_size, tm_size, rows_dev, tile_cols, col_slice)
    small_split = small_turn.reshape(2, 2, NT, blen_size, tile_cols)
    section_two = jnp.einsum("acnpv,cptrvj->antrj", small_split, landed, precision=highest)
    twist_cv = cos_twist.reshape(NT, tm_size, 1, col_slice)
    twist_sv = sin_twist.reshape(NT, tm_size, 1, col_slice)
    turned_rows = jnp.stack(
        [
            section_two[0] * twist_cv - section_two[1] * twist_sv,
            section_two[0] * twist_sv + section_two[1] * twist_cv,
        ]
    )
    real_turn = jnp.stack([cos_tile, -sin_tile]).reshape(2, tile_side, tm_size, col_slice)
    image_rows = jnp.einsum("cmtj,cntrj->rmn", real_turn, turned_rows, precision=highest)
    gradient = image_rows.reshape(rows_dev, NPIX) / NPIX
    return (gradient, weighted_residual)


def solution(mesh):
    in_specs = (
        P(("blen", "tm"), None, None, None),
        P(None, ("blen", "tm")),
        P(("blen", "tm")),
        P(("blen", "tm")),
        P(None, ("blen", "tm")),
        P(None, ("blen", "tm")),
        P(("blen", "tm"), None),
    )
    out_specs = (P(("blen", "tm"), None), P(None, ("blen", "tm")))
    return jax.shard_map(
        on_device, mesh=mesh, in_specs=in_specs, out_specs=out_specs, check_vma=False
    )
```

profile of v0, /device:TPU:0, one launch (start us, length us, event | category | flops | bytes accessed | tf_op | source)
XLA Modules:
  0.0 1047.1 jit_solution(14593329809357333968)
XLA Ops:
  3.0 4.4 sort.17
  14.8 7.3 all-to-all-start.1
  27.3 3.0 all-to-all-done.1
  30.3 2.8 all-to-all-start
  33.3 7.1 all-to-all-done
  43.2 5.3 multiply_reduce_fusion
  48.5 7.2 convolution_bitcast_fusion
  55.7 25.1 %copy.78 = f32[8,2,512,512]{3,1,0,2:T(2,128)} copy(f32[8,2,512,512]{2,3,1,0:T(8,128)} %convolution_bitcast_fusion) | data formatting | bytes 33554432 | tf_op jit(solution)/shard_map/while/body/eval_jaxpr/qrj,qrci->qcji/transpose | solution.py:94
  80.8 6.0 all-to-all-start.2
  87.2 3.9 fusion.60
  91.0 4.1 fusion.58
  97.8 173.0 %all-to-all-done.2 = f32[8,2,512,512]{3,1,0,2:T(2,128)} async-done(((f32[8,2,512,512]{3,1,0,2:T(2,128)}), f32[8,2,512,512]{3,1,0,2:T(2,128)}, u32[]{:S(2)}, u32[]{:S(2)}) %all-to-all-start.2) | async-done | bytes 16777248 | tf_op jit(solution)/shard_map/all_to_all | solution.py:110
  270.8 2.6 all-to-all-start.4
  273.4 11.0 %copy.79 = f32[8,2,512,512]{3,2,1,0:T(8,128)S(1)} copy(f32[8,2,512,512]{3,1,0,2:T(2,128)} %all-to-all-done.2) | data formatting | bytes 33554432 | tf_op jit(solution)/shard_map/all_to_all | solution.py:110
  284.4 6.7 copy.80
  291.1 42.0 %fusion.11 = f32[2,16,4,64,512]{4,1,3,2,0:T(8,128)} fusion(f32[16,4,2,64,512]{4,3,2,1,0:T(8,128)} %bitcast.109, f32[1,2,16,16]{3,2,1,0:T(8,128)S(1)} %get-tuple-element.44, f32[1,2,16,16]{3,2,1,0:T(8,128)S(1)} %get-tuple-element.43), kind=kOutput, calls=%fused_computation.23 | convolution fusion | flops 1610613760 | bytes 33558528 | tf_op jit(solution)/shard_map/acnt,tvcji->anvji/dot_general | solution.py:119
  333.1 7.1 multiply_subtract_fusion.1
  340.2 6.4 pad_maximum_fusion
  346.6 67.2 %fusion.14 = f32[2,512,16,4,64]{1,4,3,2,0:T(8,128)} fusion(f32[2,16,4,64,512]{4,1,3,2,0:T(8,128)} %pad_maximum_fusion, f32[1,2,512,512]{3,2,1,0:T(8,128)S(1)} %copy-done, f32[1,2,512,512]{3,2,1,0:T(8,128)S(1)} %get-tuple-element.34), kind=kOutput, calls=%fused_computation.24 | convolution fusion | flops 51540656128 | bytes 37748736 | tf_op jit(solution)/shard_map/acmi,cnvji->amnvj/dot_general | solution.py:128
  413.8 31.1 %copy.83 = f32[2,512,16,4,64]{4,3,2,1,0:T(4,128)} copy(f32[2,512,16,4,64]{1,4,3,2,0:T(8,128)} %fusion.14) | data formatting | bytes 33554432 | tf_op jit(solution)/shard_map/acmi,cnvji->amnvj/dot_general | solution.py:128
  444.9 27.4 %reshape.436 = f32[2,1,32,65536]{3,2,0,1:T(8,128)} reshape(f32[2,512,16,4,64]{4,3,2,1,0:T(4,128)} %copy.83) | data formatting | bytes 33554432 | tf_op jit(solution)/shard_map/reshape | solution.py:131
  472.2 28.6 %copy.84 = f32[2,1,32,65536]{3,0,1,2:T(2,128)} copy(f32[2,1,32,65536]{3,2,0,1:T(8,128)} %reshape.436) | data formatting | bytes 33554432 | tf_op jit(solution)/shard_map/reshape | solution.py:131
  500.9 6.0 all-to-all-start.3
  507.1 4.2 sine_negate_fusion
  516.5 363.0 %all-to-all-done.3 = f32[2,1,32,65536]{3,0,1,2:T(2,128)} async-done(((f32[2,1,32,65536]{3,0,1,2:T(2,128)}), f32[2,1,32,65536]{3,0,1,2:T(2,128)}, u32[]{:S(2)}, u32[]{:S(2)}) %all-to-all-start.3) | async-done | bytes 16777248 | tf_op jit(solution)/shard_map/all_to_all | solution.py:132
  879.5 38.4 %reshape.487 = f32[2,4,8,256,4,64]{5,4,3,0,2,1:T(4,128)} reshape(f32[2,1,32,65536]{3,0,1,2:T(2,128)} %all-to-all-done.3) | data formatting | bytes 33554432 | tf_op jit(solution)/shard_map/reshape | solution.py:133
  918.0 30.9 %copy.86 = f32[2,4,8,256,4,64]{3,4,1,0,5,2:T(4,128)} copy(f32[2,4,8,256,4,64]{5,4,3,0,2,1:T(4,128)} %reshape.487) | data formatting | bytes 33554432 | tf_op jit(solution)/shard_map/reshape | solution.py:133
  948.8 31.8 %fusion.17 = f32[2,16,8,256,64]{3,1,4,2,0:T(8,128)S(1)} fusion(f32[2,4,8,256,4,64]{3,4,1,0,5,2:T(4,128)} %copy.86, f32[2,2,16,4,4,1,1]{2,4,3,1,6,5,0:T(4,128)S(1)} %maximum_bitcast_fusion.17), kind=kOutput, calls=%fused_computation.25 | convolution fusion | flops 1610612736 | bytes 33558528 | tf_op jit(solution)/shard_map/acnpv,cptrvj->antrj/dot_general | solution.py:135
  980.6 2.8 multiply_subtract_fusion
  985.2 42.3 %fusion.10 = f32[256,512,16]{1,0,2:T(8,128)} fusion(f32[2,16,8,256,64]{3,1,4,2,0:T(8,128)S(1)} %pad_maximum_fusion.1, f32[1,512,8,64]{1,3,2,0:T(8,128)S(1)} %get-tuple-element.56, f32[1,512,8,64]{1,3,2,0:T(8,128)S(1)} %get-tuple-element.57), kind=kOutput, calls=%fused_computation.18 | convolution fusion | flops 25772425216 | bytes 27262976 | tf_op jit(solution)/shard_map/cmtj,cntrj->rmn/dot_general | solution.py:145
  1027.6 10.3 copy.88
  1037.9 8.9 copy.92
  (60 shorter events, 28.0 us)
Async XLA Ops:
  11.4 14.1 %copy-start.1 = (s32[512]{0:T(512)}, s32[512]{0:T(512)S(1)}, u32[]{:S(2)}) copy-start(s32[512]{0:T(512)S(1)} %compare_select_fusion) | copy-start | bytes 6148
  14.8 15.5 %all-to-all-start.1 = ((s32[2,8,32,4]{1,3,0,2:T(4,128)}), s32[2,8,32,4]{1,3,0,2:T(4,128)S(1)}, u32[]{:S(2)}, u32[]{:S(2)}) async-start(s32[2,8,32,4]{1,3,0,2:T(4,128)} %copy.70), calls=%async_computation.1 | async-start | bytes 262144 | tf_op jit(solution)/shard_map/all_to_all | solution.py:69
  30.3 10.1 all-to-all-start
  80.8 190.0 %all-to-all-start.2 = ((f32[8,2,512,512]{3,1,0,2:T(2,128)}), f32[8,2,512,512]{3,1,0,2:T(2,128)}, u32[]{:S(2)}, u32[]{:S(2)}) async-start(f32[8,2,512,512]{3,1,0,2:T(2,128)} %copy.78), calls=%async_computation.2 | async-start | bytes 33554432 | tf_op jit(solution)/shard_map/all_to_all | solution.py:110
  270.8 230.0 %all-to-all-start.4 = ((f32[2,8,32,4]{1,3,0,2:T(4,128)}), f32[2,8,32,4]{1,3,0,2:T(4,128)S(1)}, u32[]{:S(2)}, u32[]{:S(2)}) async-start(f32[2,8,32,4]{1,3,0,2:T(4,128)} %copy.90), calls=%async_computation.4 | async-start | bytes 262144 | tf_op jit(solution)/shard_map/all_to_all | solution.py:102
  340.2 6.4 copy-start
  500.9 6.0 copy-start.2
  500.9 378.7 %all-to-all-start.3 = ((f32[2,1,32,65536]{3,0,1,2:T(2,128)}), f32[2,1,32,65536]{3,0,1,2:T(2,128)}, u32[]{:S(2)}, u32[]{:S(2)}) async-start(f32[2,1,32,65536]{3,0,1,2:T(2,128)} %copy.84), calls=%async_computation.3 | async-start | bytes 33554432 | tf_op jit(solution)/shard_map/all_to_all | solution.py:132
where the time goes:
time: 1060 us; the launch traced here: 1050 us
  waiting for transfers between devices  546 us (52%)
  local copies, waits for them, and re-layouts  235 us (22%)
  matrix products  196 us (18%)
  other arithmetic  44 us (4%)
  starting transfers between devices  24.7 us (2%)
    all_to_all x1, waiting for transfers between devices, on_device(): lax.all_to_all(packed, ('blen', 'tm'), split_axis=2, concat_axis=1, tiled...  363 us
    all_to_all x1, waiting for transfers between devices, on_device(): lax.all_to_all(adjoint, 'tm', split_axis=2, concat_axis=0, tiled=True)  173 us
    reshape x2, local copies, waits for them, and re-layouts, on_device(): landed.reshape(2, blen_size, tm_size, rows_dev, tile_cols, col_slice)  69.3 us
    dot_general x1, matrix products, on_device(): jnp.einsum('acmi,cnvji->amnvj', tile_turn, turned, precision=highest)  67.2 us
    reshape x2, local copies, waits for them, and re-layouts, on_device(): packed = columns.reshape(2, 1, devices, spread_cols)  56 us
    dot_general x1, matrix products, on_device(): jnp.einsum('cmtj,cntrj->rmn', real_turn, turned_rows, precision=highest)  42.3 us
    dot_general x1, matrix products, on_device(): jnp.einsum('acnt,tvcji->anvji', small_turn, pieces, precision=highest)  42 us
    dot_general x1, matrix products, on_device(): jnp.einsum('acnpv,cptrvj->antrj', small_split, landed, precision=highest)  31.8 us
  transfers between devices with their start and end apart: 5, of which 4 were waited for; matrix products, arithmetic and copies ran while one was open for 24% of the time, Pallas kernels for 0%

commit v1 on v0

--- a/solution.py
+++ b/solution.py
@@ -10,6 +10,29 @@
 MOST = 4
 kernel_scale = 0.5
 highest = lax.Precision.HIGHEST
+
+
+def in_blocks(value, dim, size):
+    shape = value.shape
+    tiles = value.reshape(*shape[:dim], size, shape[dim] // size, *shape[dim + 1 :])
+    return jnp.moveaxis(tiles, dim, 0)
+
+
+def joined_along(blocks, dim):
+    blocks = jnp.moveaxis(blocks, 0, dim)
+    shape = blocks.shape
+    return blocks.reshape(*shape[:dim], shape[dim] * shape[dim + 1], *shape[dim + 2 :])
+
+
+def exchange_in_pairs(value, axis, split_dim, concat_dim):
+    peers, here = (lax.axis_size(axis), lax.axis_index(axis))
+    blocks = in_blocks(value, split_dim, peers)
+    done = [blocks[here]]
+    for step in range(1, peers):
+        sent = blocks[here ^ step]
+        done.append(lax.ppermute(sent, axis, [(i, i ^ step) for i in range(peers)]))
+    blocks = jnp.stack(done)[here ^ jnp.arange(peers)]
+    return joined_along(blocks, concat_dim)
 
 
 def taps_full(offsets, fractions, tile_side):
@@ -107,7 +130,7 @@
         tiled=True,
     )
     weighted_residual = returned.reshape(2, total_slots)[:, slot_of]
-    relaid = lax.all_to_all(adjoint, "tm", split_axis=2, concat_axis=0, tiled=True)
+    relaid = exchange_in_pairs(adjoint, "tm", 2, 0)
     tile_cols = NT // blen_size
     col_slice = tile_side // tm_size
     pieces = relaid.reshape(NT, tile_cols, 2, col_slice, tile_side)

time: 1060 us -> 1050 us (level)
  waiting for transfers between devices: 546 us -> 528 us
    all_to_all x1 -> x0, waiting for transfers between devices: 173 us -> none  [on_device(): lax.all_to_all(adjoint, 'tm', split_axis=2, concat_axis=0, tiled=True)]
    ppermute x0 -> x7, waiting for transfers between devices: none -> 155 us  [exchange_in_pairs(): done.append(lax.ppermute(sent, axis, [(i, i ^ step) for i in range(peers)]))]
    transpose x1 -> x0, local copies, waits for them, and re-layouts: 25.1 us -> none  [grid_step(): jnp.einsum('qrj,qrci->qcji', taps_v, spread, preferred_element_type=jnp.f...]
    unnamed x11 -> x16, local copies, waits for them, and re-layouts: 12.5 us -> 34.6 us
    all_to_all x2 -> x0, local copies, waits for them, and re-layouts: 17.7 us -> none  [on_device(): lax.all_to_all(adjoint, 'tm', split_axis=2, concat_axis=0, tiled=True)]
    gather x0 -> x1, local copies, waits for them, and re-layouts: none -> 13.7 us  [exchange_in_pairs(): blocks = jnp.stack(done)[here ^ jnp.arange(peers)]]
    squeeze x0 -> x1, local copies, waits for them, and re-layouts: none -> 11.1 us  [exchange_in_pairs(): sent = blocks[here ^ step]]
  transfers between devices with their start and end apart: 5 -> 11, of which waited for: 4 -> 6; matrix products, arithmetic and copies ran while one was open for 24% -> 26% of each run, Pallas kernels for 0% -> 0%
where the time goes in v1:
time: 1050 us; the launch traced here: 1040 us
  waiting for transfers between devices  528 us (50%)
  local copies, waits for them, and re-layouts  243 us (23%)
  matrix products  196 us (19%)
  other arithmetic  46.2 us (4%)
  starting transfers between devices  21.1 us (2%)
    all_to_all x1, waiting for transfers between devices, on_device(): lax.all_to_all(packed, ('blen', 'tm'), split_axis=2, concat_axis=1, tiled...  363 us
    ppermute x7, waiting for transfers between devices, exchange_in_pairs(): done.append(lax.ppermute(sent, axis, [(i, i ^ step) for i in range(peers)]))  155 us
    reshape x2, local copies, waits for them, and re-layouts, on_device(): landed.reshape(2, blen_size, tm_size, rows_dev, tile_cols, col_slice)  69.3 us
    dot_general x1, matrix products, on_device(): jnp.einsum('acmi,cnvji->amnvj', tile_turn, turned, precision=highest)  67 us
    reshape x2, local copies, waits for them, and re-layouts, on_device(): packed = columns.reshape(2, 1, devices, spread_cols)  56 us
    dot_general x1, matrix products, on_device(): jnp.einsum('cmtj,cntrj->rmn', real_turn, turned_rows, precision=highest)  42.3 us
    dot_general x1, matrix products, on_device(): jnp.einsum('acnt,tvcji->anvji', small_turn, pieces, precision=highest)  42 us
    unnamed x16, local copies, waits for them, and re-layouts  34.6 us
  transfers between devices with their start and end apart: 11, of which 6 were waited for; matrix products, arithmetic and copies ran while one was open for 26% of the time, Pallas kernels for 0%

profile of v1, /device:TPU:0, one launch (start us, length us, event | category | flops | bytes accessed | tf_op | source)
XLA Modules:
  0.0 1035.6 jit_solution(9201545138206474838)
XLA Ops:
  3.0 4.4 sort.17
  14.8 7.3 all-to-all-start.1
  33.3 7.1 all-to-all-done
  46.3 5.5 multiply_reduce_fusion
  51.8 7.3 fusion.30
  59.1 11.1 %dynamic-slice_bitcast_fusion = (f32[8,2,64,512]{3,2,1,0:T(8,128)S(1)}, f32[8,2,64,512]{3,2,1,0:T(8,128)}, f32[8,2,64,512]{3,2,1,0:T(8,128)}, f32[8,2,64,512]{3,...) fusion(f32[8,2,8,64,512]{4,3,2,1,0:T(8,128)} %bitcast.142, ...), kind=kLoop, calls=%fused_computation.53 | loop fusion | bytes 29360156 | tf_op jit(solution)/shard_map/squeeze | solution.py:32
  72.4 3.9 fusion.61
  76.9 4.1 fusion.59
  89.0 31.1 %collective-permute-done.1 = f32[8,2,64,512]{3,2,1,0:T(8,128)} collective-permute-done((f32[8,2,64,512]{3,2,1,0:T(8,128)}, f32[8,2,64,512]{3,2,1,0:T(8,128)}, u32[]{:S(2)}, u32[]{:S(2)}) %collective-permute-start.1) | collective-permute-done | bytes 2097184 | tf_op jit(solution)/shard_map/ppermute | solution.py:33
  120.1 3.2 bitcast_dynamic-update-slice_fusion.7
  129.5 34.5 %collective-permute-done.2 = f32[8,2,64,512]{3,2,1,0:T(8,128)} collective-permute-done((f32[8,2,64,512]{3,2,1,0:T(8,128)}, f32[8,2,64,512]{3,2,1,0:T(8,128)}, u32[]{:S(2)}, u32[]{:S(2)}) %collective-permute-start.2) | collective-permute-done | bytes 2097184 | tf_op jit(solution)/shard_map/ppermute | solution.py:33
  164.1 3.2 bitcast_dynamic-update-slice_fusion.4
  167.3 3.2 bitcast_dynamic-update-slice_fusion.3
  170.5 89.6 %collective-permute-done.4 = f32[8,2,64,512]{3,2,1,0:T(8,128)} collective-permute-done((f32[8,2,64,512]{3,2,1,0:T(8,128)}, f32[8,2,64,512]{3,2,1,0:T(8,128)}, u32[]{:S(2)}, u32[]{:S(2)}) %collective-permute-start.4) | collective-permute-done | bytes 2097184 | tf_op jit(solution)/shard_map/ppermute | solution.py:33
  263.2 3.2 bitcast_dynamic-update-slice_fusion.1
  267.9 13.7 %gather_fusion = f32[8,8,2,64,512]{4,3,2,1,0:T(8,128)} fusion(f32[8,8,2,64,512]{4,3,2,1,0:T(8,128)} %bitcast_dynamic-update-slice_fusion, s32[1024]{0:T(1024)S(1)} %pad_clamp_fusion.1), kind=kCustom, calls=%fused_computation | custom fusion | bytes 33554464 | tf_op jit(solution)/shard_map/gather | solution.py:34
  281.6 42.0 %fusion.11 = f32[2,16,4,64,512]{4,1,3,2,0:T(8,128)} fusion(f32[16,4,2,64,512]{4,3,2,1,0:T(8,128)} %bitcast.144, f32[1,2,16,16]{3,2,1,0:T(8,128)S(1)} %get-tuple-element.51, f32[1,2,16,16]{3,2,1,0:T(8,128)S(1)} %get-tuple-element.50), kind=kOutput, calls=%fused_computation.23 | convolution fusion | flops 1610613760 | bytes 33558528 | tf_op jit(solution)/shard_map/acnt,tvcji->anvji/dot_general | solution.py:142
  323.6 7.1 multiply_subtract_fusion.1
  330.8 6.6 pad_maximum_fusion
  337.3 67.0 %fusion.14 = f32[2,512,16,4,64]{1,4,3,2,0:T(8,128)} fusion(f32[2,16,4,64,512]{4,1,3,2,0:T(8,128)} %pad_maximum_fusion, f32[1,2,512,512]{3,2,1,0:T(8,128)S(1)} %copy-done.1, f32[1,2,512,512]{3,2,1,0:T(8,128)S(1)} %copy-done), kind=kOutput, calls=%fused_computation.24 | convolution fusion | flops 51540656128 | bytes 37748736 | tf_op jit(solution)/shard_map/acmi,cnvji->amnvj/dot_general | solution.py:151
  404.3 31.1 %copy.79 = f32[2,512,16,4,64]{4,3,2,1,0:T(4,128)} copy(f32[2,512,16,4,64]{1,4,3,2,0:T(8,128)} %fusion.14) | data formatting | bytes 33554432 | tf_op jit(solution)/shard_map/acmi,cnvji->amnvj/dot_general | solution.py:151
  435.4 27.4 %reshape.466 = f32[2,1,32,65536]{3,2,0,1:T(8,128)} reshape(f32[2,512,16,4,64]{4,3,2,1,0:T(4,128)} %copy.79) | data formatting | bytes 33554432 | tf_op jit(solution)/shard_map/reshape | solution.py:154
  462.7 28.6 %copy.80 = f32[2,1,32,65536]{3,0,1,2:T(2,128)} copy(f32[2,1,32,65536]{3,2,0,1:T(8,128)} %reshape.466) | data formatting | bytes 33554432 | tf_op jit(solution)/shard_map/reshape | solution.py:154
  491.3 3.9 all-to-all-start.2
  495.5 4.2 sine_negate_fusion
  504.9 363.1 %all-to-all-done.2 = f32[2,1,32,65536]{3,0,1,2:T(2,128)} async-done(((f32[2,1,32,65536]{3,0,1,2:T(2,128)}), f32[2,1,32,65536]{3,0,1,2:T(2,128)}, u32[]{:S(2)}, u32[]{:S(2)}) %all-to-all-start.2) | async-done | bytes 16777248 | tf_op jit(solution)/shard_map/all_to_all | solution.py:155
  868.0 38.4 %reshape.526 = f32[2,4,8,256,4,64]{5,4,3,0,2,1:T(4,128)} reshape(f32[2,1,32,65536]{3,0,1,2:T(2,128)} %all-to-all-done.2) | data formatting | bytes 33554432 | tf_op jit(solution)/shard_map/reshape | solution.py:156
  906.4 30.9 %copy.82 = f32[2,4,8,256,4,64]{3,4,1,0,5,2:T(4,128)} copy(f32[2,4,8,256,4,64]{5,4,3,0,2,1:T(4,128)} %reshape.526) | data formatting | bytes 33554432 | tf_op jit(solution)/shard_map/reshape | solution.py:156
  937.3 31.8 %fusion.17 = f32[2,16,8,256,64]{3,1,4,2,0:T(8,128)S(1)} fusion(f32[2,4,8,256,4,64]{3,4,1,0,5,2:T(4,128)} %copy.82, f32[2,2,16,4,4,1,1]{2,4,3,1,6,5,0:T(4,128)S(1)} %maximum_bitcast_fusion.17), kind=kOutput, calls=%fused_computation.25 | convolution fusion | flops 1610612736 | bytes 33558528 | tf_op jit(solution)/shard_map/acnpv,cptrvj->antrj/dot_general | solution.py:158
  973.7 42.3 %fusion.10 = f32[256,512,16]{1,0,2:T(8,128)} fusion(f32[2,16,8,256,64]{3,1,4,2,0:T(8,128)S(1)} %pad_maximum_fusion.1, f32[1,512,8,64]{1,3,2,0:T(8,128)S(1)} %get-tuple-element.63, f32[1,512,8,64]{1,3,2,0:T(8,128)S(1)} %get-tuple-element.64), kind=kOutput, calls=%fused_computation.18 | convolution fusion | flops 25772425216 | bytes 27262976 | tf_op jit(solution)/shard_map/cmtj,cntrj->rmn/dot_general | solution.py:168
  1016.0 10.3 copy.84
  1026.3 8.9 copy.88
  (80 shorter events, 58.5 us)
Async XLA Ops:
  14.8 15.5 %all-to-all-start.1 = ((s32[2,8,32,4]{1,3,0,2:T(4,128)}), s32[2,8,32,4]{1,3,0,2:T(4,128)S(1)}, u32[]{:S(2)}, u32[]{:S(2)}) async-start(s32[2,8,32,4]{1,3,0,2:T(4,128)} %copy.68), calls=%async_computation.1 | async-start | bytes 262144 | tf_op jit(solution)/shard_map/all_to_all | solution.py:92
  30.3 10.1 all-to-all-start
  70.2 14.7 %collective-permute-start = (f32[8,2,64,512]{3,2,1,0:T(8,128)}, f32[8,2,64,512]{3,2,1,0:T(8,128)}, u32[]{:S(2)}, u32[]{:S(2)}) collective-permute-start(f32[8,2,64,512]{3,2,1,0:T(8,128)} %get-tuple-element.40), channel_id=1, source_target_pairs={{0,1},{1,0},{2,3},{3,2},{4,5},{5,4},{6,7},{7,6},{8,9},{9,8},{10,11... | collective-permute-start | bytes 6291464 | tf_op jit(solution)/shard_map/ppermute | solution.py:33
  70.3 49.8 %collective-permute-start.1 = (f32[8,2,64,512]{3,2,1,0:T(8,128)}, f32[8,2,64,512]{3,2,1,0:T(8,128)}, u32[]{:S(2)}, u32[]{:S(2)}) collective-permute-start(f32[8,2,64,512]{3,2,1,0:T(8,128)} %get-tuple-element.39), channel_id=1, source_target_pairs={{0,2},{1,3},{2,0},{3,1},{4,6},{5,7},{6,4},{7,5},{8,10},{9,11},{10,... | collective-permute-start | bytes 6291464 | tf_op jit(solution)/shard_map/ppermute | solution.py:33
  70.8 93.2 %collective-permute-start.2 = (f32[8,2,64,512]{3,2,1,0:T(8,128)}, f32[8,2,64,512]{3,2,1,0:T(8,128)}, u32[]{:S(2)}, u32[]{:S(2)}) collective-permute-start(f32[8,2,64,512]{3,2,1,0:T(8,128)} %get-tuple-element.38), channel_id=1, source_target_pairs={{0,3},{1,2},{2,1},{3,0},{4,7},{5,6},{6,5},{7,4},{8,11},{9,10},{10,... | collective-permute-start | bytes 6291464 | tf_op jit(solution)/shard_map/ppermute | solution.py:33
  76.3 91.0 %collective-permute-start.3 = (f32[8,2,64,512]{3,2,1,0:T(8,128)}, f32[8,2,64,512]{3,2,1,0:T(8,128)}, u32[]{:S(2)}, u32[]{:S(2)}) collective-permute-start(f32[8,2,64,512]{3,2,1,0:T(8,128)} %get-tuple-element.37), channel_id=1, source_target_pairs={{0,4},{1,5},{2,6},{3,7},{4,0},{5,1},{6,2},{7,3},{8,12},{9,13},{10,... | collective-permute-start | bytes 6291464 | tf_op jit(solution)/shard_map/ppermute | solution.py:33
  81.0 179.0 %collective-permute-start.4 = (f32[8,2,64,512]{3,2,1,0:T(8,128)}, f32[8,2,64,512]{3,2,1,0:T(8,128)}, u32[]{:S(2)}, u32[]{:S(2)}) collective-permute-start(f32[8,2,64,512]{3,2,1,0:T(8,128)} %get-tuple-element.36), channel_id=1, source_target_pairs={{0,5},{1,4},{2,7},{3,6},{4,1},{5,0},{6,3},{7,2},{8,13},{9,12},{10,... | collective-permute-start | bytes 6291464 | tf_op jit(solution)/shard_map/ppermute | solution.py:33
  84.9 178.3 %collective-permute-start.5 = (f32[8,2,64,512]{3,2,1,0:T(8,128)}, f32[8,2,64,512]{3,2,1,0:T(8,128)}, u32[]{:S(2)}, u32[]{:S(2)}) collective-permute-start(f32[8,2,64,512]{3,2,1,0:T(8,128)} %get-tuple-element.35), channel_id=1, source_target_pairs={{0,6},{1,7},{2,4},{3,5},{4,2},{5,3},{6,0},{7,1},{8,14},{9,15},{10,... | collective-permute-start | bytes 6291464 | tf_op jit(solution)/shard_map/ppermute | solution.py:33
  86.3 405.1 %all-to-all-start.3 = ((f32[2,8,32,4]{1,3,0,2:T(4,128)}), f32[2,8,32,4]{1,3,0,2:T(4,128)S(1)}, u32[]{:S(2)}, u32[]{:S(2)}) async-start(f32[2,8,32,4]{1,3,0,2:T(4,128)} %copy.86), calls=%async_computation.3 | async-start | bytes 262144 | tf_op jit(solution)/shard_map/all_to_all | solution.py:125
  120.1 146.2 %collective-permute-start.6 = (f32[8,2,64,512]{3,2,1,0:T(8,128)S(1)}, f32[8,2,64,512]{3,2,1,0:T(8,128)S(1)}, u32[]{:S(2)}, u32[]{:S(2)}) collective-permute-start(f32[8,2,64,512]{3,2,1,0:T(8,128)S(1)} %get-tuple-element.34), channel_id=1, source_target_pairs={{0,7},{1,6},{2,5},{3,4},{4,3},{5,2},{6,1},{7,0},{8,15},{9,14},{10,... | collective-permute-start | bytes 6291464 | tf_op jit(solution)/shard_map/ppermute | solution.py:33
  330.7 6.6 copy-start
  330.7 6.6 copy-start.1
  491.3 376.7 %all-to-all-start.2 = ((f32[2,1,32,65536]{3,0,1,2:T(2,128)}), f32[2,1,32,65536]{3,0,1,2:T(2,128)}, u32[]{:S(2)}, u32[]{:S(2)}) async-start(f32[2,1,32,65536]{3,0,1,2:T(2,128)} %copy.80), calls=%async_computation.2 | async-start | bytes 33554432 | tf_op jit(solution)/shard_map/all_to_all | solution.py:155
